TPU v7x, 128 devices: a whole 4x4x4 slice. The times are simulated.
128 devices in a mesh: rows: 8 (over z_hi, y), cols: 16 (over z_lo, x, core).
Axes of the slice: x: 4, y: 4, z: 4 (z_hi: 2, z_lo: 2; z = z_hi * 2 + z_lo), core: 2. Of those that a mesh axis runs over, the one named last changes fastest.
Arguments:
- dosage: int32 [512, 24576], P('cols', 'rows'), may hold values from 0 to 2
- present: int32 [512, 24576], P('cols', 'rows'), may hold values from 0 to 1, as said below
- components: float32 [32, 24576], P(None, 'rows'), may hold values from -8 to 8
Outputs:
- kinship: float32 [24576, 24576], P('rows', 'cols')
Inputs may be any that keep to these rules, and one draw needn't show every extreme that they name: `present`: markers whose index is a multiple of 8 are observed for every person.
All inputs are finite; a program needn't handle non-finite values.
Results may differ from a plain program's by a relative error of at most 0.0036.
Values may be sent and summed in bfloat16 or wider, within the bound.
A program may use at most 128 MiB of HBM per device.

v0:
```python
import jax
import jax.numpy as jnp
from jax import lax
from jax.sharding import PartitionSpec as P


def broadcast(block, axis, holder):
    block = jnp.where(lax.axis_index(axis) == holder, block, jnp.zeros_like(block))
    return lax.psum(block, axis)


def solve_normal(gram, moment):
    width = gram.shape[0]
    index_col = jnp.arange(width, dtype=jnp.int32)[:, None]
    columns = []
    for j in range(width):
        column = gram[:, j, :]
        if j > 0:
            stacked = jnp.stack(columns, axis=1)
            column = column - jnp.sum(stacked * stacked[j][None, :, :], axis=1)
        pivot = jnp.sqrt(column[j])
        columns.append(jnp.where(index_col >= j, column / pivot[None, :], jnp.zeros_like(column)))
    factor = jnp.stack(columns, axis=1)
    forward = []
    for j in range(width):
        value = moment[j]
        for k in range(j):
            value = value - factor[j, k] * forward[k]
        forward.append(value / factor[j, j])
    backward = [None] * width
    for j in range(width - 1, -1, -1):
        value = forward[j]
        for k in range(j + 1, width):
            value = value - factor[k, j] * backward[k]
        backward[j] = value / factor[j, j]
    return jnp.stack(backward, axis=0)


def per_device(dosage, present, components):
    people = components.shape[1]
    design = jnp.concatenate([jnp.ones((1, people), jnp.float32), components], axis=0)
    width = design.shape[0]
    observed = present.astype(jnp.float32)
    counts = dosage.astype(jnp.float32)
    target = 0.5 * counts * observed
    outer_rows = (design[:, None, :] * design[None, :, :]).reshape(width * width, people)
    gram_part = jnp.dot(
        outer_rows, observed.T, precision=lax.Precision.HIGHEST, preferred_element_type=jnp.float32
    )
    moment_part = jnp.dot(
        design, target.T, precision=lax.Precision.HIGHEST, preferred_element_type=jnp.float32
    )
    gram_flat, moment = lax.psum((gram_part, moment_part), "rows")
    markers_here = observed.shape[0]
    gram = gram_flat.reshape(width, width, markers_here)
    coef = solve_normal(gram, moment)
    fitted = jnp.dot(
        coef.T, design, precision=lax.Precision.HIGHEST, preferred_element_type=jnp.float32
    )
    freq = jnp.clip(fitted, 0.01, 0.99)
    resid = observed * (counts - 2.0 * freq)
    sdev = observed * jnp.sqrt(freq * (1.0 - freq))
    panel = jnp.stack([resid, sdev]).astype(jnp.bfloat16)
    ratio = lax.axis_size("cols") // lax.axis_size("rows")
    column_width = people // ratio
    col_index = lax.axis_index("cols")
    col_start = col_index % ratio * column_width
    owner = col_index // ratio
    contract = (((0,), (0,)), ((), ()))
    full_rows = lax.all_gather(panel, "cols", axis=1, tiled=True)
    own_part = lax.dynamic_slice_in_dim(full_rows, col_start, column_width, 2)
    full_cols = broadcast(own_part, "rows", owner)
    numer = lax.dot_general(
        full_rows[0], full_cols[0], contract, preferred_element_type=jnp.float32
    )
    denom = lax.dot_general(
        full_rows[1], full_cols[1], contract, preferred_element_type=jnp.float32
    )
    return numer / (4.0 * denom)


def solution(mesh):
    placed = (P("cols", "rows"), P("cols", "rows"), P(None, "rows"))
    return jax.shard_map(
        per_device, mesh=mesh, in_specs=placed, out_specs=P("rows", "cols"), check_vma=False
    )
```

profile of v0, /device:TPU:0, one launch (start us, length us, event | category | flops | bytes accessed | tf_op | source)
XLA Modules:
  0.0 338.4 jit_solution(12750329239006864521)
XLA Ops:
  6.5 1.0 concatenate.3
  7.6 8.0 %broadcast_multiply_fusion = f32[33,33,3072]{2,1,0:T(8,128)} fusion(f32[33,3072]{1,0:T(8,128)S(1)} %concatenate.3), kind=kLoop, calls=%fused_computation.1 | loop fusion | flops 3345408 | bytes 13787136 | tf_op jit(solution)/shard_map/mul | solution.py:46
  15.6 10.5 %mul.11354 = f32[1089,3072]{1,0:T(8,128)} reshape(f32[33,33,3072]{2,1,0:T(8,128)} %broadcast_multiply_fusion) | data formatting | bytes 26763264 | tf_op jit(solution)/shard_map/mul | solution.py:46
  26.1 14.2 %fusion.8 = f32[1089,32]{0,1:T(8,128)S(1)} fusion(f32[1089,3072]{1,0:T(8,128)} %mul.11354, s32[32,3072]{1,0:T(8,128)S(1)} %copy-done.1), kind=kOutput, calls=%fused_computation.550 | convolution fusion | flops 1284734976 | bytes 13914240 | tf_op jit(solution)/shard_map/dot_general | solution.py:47
  40.6 1.2 copy.48
  43.4 42.9 %psum.21 = f32[33,32]{1,0:T(8,128)S(1)} all-reduce(f32[33,32]{1,0:T(8,128)S(1)} %fusion.4), channel_id=1, replica_groups=mesh['rows'=8,'cols'=16] {'rows'}, use_global_device_ids=true, to_apply=%region_0.0 | all-reduce | flops 1056 | bytes 8448 | tf_op jit(solution)/shard_map/psum | solution.py:53
  86.4 44.7 %all-reduce.4.cloned.1.call-done = f32[33,33,32]{2,0,1:T(8,128)} async-done(((f32[33,33,32]{2,0,1:T(8,128)}), f32[33,33,32]{2,0,1:T(8,128)}) %all-reduce.4.cloned.1.call-update) | async-done | bytes 139408 | tf_op jit(solution)/shard_map/psum | solution.py:53
  135.0 0.8 constant_dynamic-update-slice_fusion.79
  136.7 0.8 constant_dynamic-update-slice_fusion.514
  138.4 0.8 constant_dynamic-update-slice_fusion.513
  140.1 0.8 constant_dynamic-update-slice_fusion.512
  141.8 0.8 constant_dynamic-update-slice_fusion.511
  143.5 0.8 constant_dynamic-update-slice_fusion.510
  145.2 0.8 constant_dynamic-update-slice_fusion.509
  146.9 0.8 constant_dynamic-update-slice_fusion.508
  148.6 0.8 constant_dynamic-update-slice_fusion.507
  157.1 0.8 fusion.144
  158.4 0.8 subtract_divide_fusion
  160.1 0.8 pad_maximum_fusion
  161.2 40.2 %all-gather.2.cloned.1.call-done = bf16[2,512,3072]{2,1,0:T(8,128)(2,1)} async-done(((bf16[2,32,3072]{2,1,0:T(8,128)(2,1)}), bf16[2,512,3072]{2,1,0:T(8,128)(2,1)}) %all-gather.2.cloned.1.call-update) | async-done | bytes 6291472 | tf_op jit(solution)/shard_map/all_gather | solution.py:70
  201.4 4.1 %dynamic-slice_select_fusion = bf16[2,512,1536]{2,1,0:T(8,128)(2,1)} fusion(bf16[2,512,3072]{2,1,0:T(8,128)(2,1)} %all-gather.2.cloned.1.call-done, s32[]{:T(128)S(6)} %select_n.281, pred[]{:T(512)S(6)} %eq.5), kind=kLoop, calls=%fused_computation.6 | loop fusion | flops 1572864 | bytes 6291461 | tf_op jit(solution)/shard_map/jit(_where)/select_n | solution.py:8
  205.5 100.6 %all-reduce.6.cloned.1.call-done = bf16[2,512,1536]{2,1,0:T(8,128)(2,1)} async-done(((bf16[2,512,1536]{2,1,0:T(8,128)(2,1)}), bf16[2,512,1536]{2,1,0:T(8,128)(2,1)}) %all-reduce.6.cloned.1.call-update) | async-done | bytes 3145744 | tf_op jit(solution)/shard_map/psum | solution.py:9
  306.1 11.7 %fusion = f32[3072,1536]{1,0:T(8,128)} fusion(bf16[2,512,3072]{2,1,0:T(8,128)(2,1)} %all-gather.2.cloned.1.call-done, bf16[2,512,1536]{2,1,0:T(8,128)(2,1)} %all-reduce.6.cloned.1.call-done), kind=kOutput, calls=%fused_computation.5 | convolution fusion | flops 4831838208 | bytes 23592960 | tf_op jit(solution)/shard_map/dot_general | solution.py:73
  317.8 14.1 %multiply_divide_fusion = f32[3072,1536]{1,0:T(8,128)} fusion(f32[3072,1536]{1,0:T(8,128)} %fusion, bf16[2,512,3072]{2,1,0:T(8,128)(2,1)} %all-gather.2.cloned.1.call-done, bf16[2,512,1536]{2,1,0:T(8,128)(2,1)S(1)} %copy-done.4), kind=kOutput, calls=%fused_computation | convolution fusion | flops 4841275392 | bytes 42467328 | tf_op jit(solution)/shard_map/dot_general | solution.py:76
  (305 shorter events, 21.0 us)
Async XLA Ops:
  6.5 124.5 %all-reduce.4.cloned.1.call-start = ((), (), s32[]{:S(2)}) async-start(), calls=%async_computation | async-start | bytes 1351680 | tf_op jit(solution)/shard_map/psum | solution.py:53
  15.6 10.6 %copy-start.1 = (s32[32,3072]{1,0:T(8,128)S(1)}, s32[32,3072]{1,0:T(8,128)}, u32[]{:S(2)}) copy-start(s32[32,3072]{1,0:T(8,128)} %param.4) | copy-start | bytes 1179652
  26.1 16.1 %copy-start = (f32[32,3072]{1,0:T(8,128)S(1)}, f32[32,3072]{1,0:T(8,128)}, u32[]{:S(2)}) copy-start(f32[32,3072]{1,0:T(8,128)} %param.5) | copy-start | bytes 1179652
  26.1 16.1 %copy-start.3 = (s32[32,3072]{1,0:T(8,128)S(1)}, s32[32,3072]{1,0:T(8,128)}, u32[]{:S(2)}) copy-start(s32[32,3072]{1,0:T(8,128)} %param.3) | copy-start | bytes 1179652
  41.8 159.6 %all-gather.2.cloned.1.call-start = ((), (), s32[]{:S(2)}) async-start(), calls=%async_computation.1 | async-start | bytes 6684672 | tf_op jit(solution)/shard_map/all_gather | solution.py:70
  131.1 18.4 %copy-start.2 = (f32[33,33,32]{2,0,1:T(8,128)S(1)}, f32[33,33,32]{2,0,1:T(8,128)}, u32[]{:S(2)}) copy-start(f32[33,33,32]{2,0,1:T(8,128)} %all-reduce.4.cloned.1.call-done) | copy-start | bytes 418180
  160.9 145.2 %all-reduce.6.cloned.1.call-start = ((), (), s32[]{:S(2)}) async-start(), calls=%async_computation.2 | async-start | bytes 6291456 | tf_op jit(solution)/shard_map/psum | solution.py:9
  306.1 11.7 %copy-start.4 = (bf16[2,512,1536]{2,1,0:T(8,128)(2,1)S(1)}, bf16[2,512,1536]{2,1,0:T(8,128)(2,1)}, u32[]{:S(2)}) copy-start(bf16[2,512,1536]{2,1,0:T(8,128)(2,1)} %all-reduce.6.cloned.1.call-done) | copy-start | bytes 9437188
Sparse Core Ops, SparseCore 0:
  41.9 89.0 all-reduce.3
  161.0 40.3 all-gather.1
  205.6 100.4 all-reduce.5
where the time goes:
time: 340 us; the launch traced here: 338 us
  waiting for transfers between devices  186 us (55%)
  blocking collectives  42.9 us (13%)
  matrix products  41.3 us (12%)
  other arithmetic  37.7 us (11%)
  local copies, waits for them, and re-layouts  16.1 us (5%)
  between operations  14.5 us (4%)
    psum x1, waiting for transfers between devices, broadcast(): return lax.psum(block, axis)  101 us
    psum x1, waiting for transfers between devices, per_device(): gram_flat, moment = lax.psum((gram_part, moment_part), 'rows')  44.7 us
    psum x1, blocking collectives, per_device(): gram_flat, moment = lax.psum((gram_part, moment_part), 'rows')  42.9 us
    all_gather x1, waiting for transfers between devices, per_device(): full_rows = lax.all_gather(panel, 'cols', axis=1, tiled=True)  40.2 us
    dot_general x1, matrix products, per_device(): jnp.dot(outer_rows, observed.T, precision=lax.Precision.HIGHEST, preferre...  14.2 us
    dot_general x1, matrix products, per_device(): lax.dot_general(full_rows[1], full_cols[1], contract, preferred_element_t...  14.1 us
    dot_general x1, matrix products, per_device(): lax.dot_general(full_rows[0], full_cols[0], contract, preferred_element_t...  11.7 us
    mul x1, local copies, waits for them, and re-layouts, per_device(): design[:, None, :] * design[None, :, :]  10.5 us
  transfers between devices with their start and end apart: 3, of which 3 were waited for; matrix products, arithmetic and copies ran while one was open for 0% of the time, Pallas kernels for 0%

commit v1 on v0

--- a/solution.py
+++ b/solution.py
@@ -67,7 +67,12 @@
     col_start = col_index % ratio * column_width
     owner = col_index // ratio
     contract = (((0,), (0,)), ((), ()))
-    full_rows = lax.all_gather(panel, "cols", axis=1, tiled=True)
+    full_rows = jnp.concatenate(
+        lax.all_to_all(
+            jnp.stack(lax.axis_size("cols") * [panel]), "cols", split_axis=0, concat_axis=0
+        ),
+        axis=1,
+    )
     own_part = lax.dynamic_slice_in_dim(full_rows, col_start, column_width, 2)
     full_cols = broadcast(own_part, "rows", owner)
     numer = lax.dot_general(

time: 340 us -> 384 us (1.13)
  waiting for transfers between devices: 186 us -> 221 us
  local copies, waits for them, and re-layouts: 16.1 us -> 30.7 us
  other arithmetic: 37.7 us -> 27.3 us
  starting transfers between devices: 0.31 us -> 4.89 us
    all_to_all x0 -> x1, waiting for transfers between devices: none -> 84.1 us  [per_device(): lax.all_to_all(jnp.stack(lax.axis_size('cols') * [panel]), 'cols', split_...]
    all_gather x1 -> x0, waiting for transfers between devices: 40.2 us -> none  [per_device(): full_rows = lax.all_gather(panel, 'cols', axis=1, tiled=True)]
    psum x1, waiting for transfers between devices: 101 us -> 92.6 us  [broadcast(): return lax.psum(block, axis)]
    slice x0 -> x1, local copies, waits for them, and re-layouts: none -> 5.19 us  [per_device(): full_rows[1]]
    all_to_all x0 -> x1, starting transfers between devices: none -> 4.63 us  [per_device(): lax.all_to_all(jnp.stack(lax.axis_size('cols') * [panel]), 'cols', split_...]
    unnamed x32, other arithmetic: 10.3 us -> 5.94 us
  transfers between devices with their start and end apart: 3 -> 3, of which waited for: 3 -> 3; matrix products, arithmetic and copies ran while one was open for 0% -> 2% of each run, Pallas kernels for 0% -> 0%
where the time goes in v1:
time: 384 us; the launch traced here: 383 us
  waiting for transfers between devices  221 us (58%)
  blocking collectives  42.9 us (11%)
  matrix products  40.4 us (11%)
  local copies, waits for them, and re-layouts  30.7 us (8%)
  other arithmetic  27.3 us (7%)
  between operations  15 us (4%)
  starting transfers between devices  4.89 us (1%)
    psum x1, waiting for transfers between devices, broadcast(): return lax.psum(block, axis)  92.6 us
    all_to_all x1, waiting for transfers between devices, per_device(): lax.all_to_all(jnp.stack(lax.axis_size('cols') * [panel]), 'cols', split_...  84.1 us
    psum x1, waiting for transfers between devices, per_device(): gram_flat, moment = lax.psum((gram_part, moment_part), 'rows')  44.7 us
    psum x1, blocking collectives, per_device(): gram_flat, moment = lax.psum((gram_part, moment_part), 'rows')  42.9 us
    dot_general x1, matrix products, per_device(): jnp.dot(outer_rows, observed.T, precision=lax.Precision.HIGHEST, preferre...  14.2 us
    dot_general x1, matrix products, per_device(): lax.dot_general(full_rows[1], full_cols[1], contract, preferred_element_t...  13.2 us
    dot_general x1, matrix products, per_device(): lax.dot_general(full_rows[0], full_cols[0], contract, preferred_element_t...  11.6 us
    mul x1, local copies, waits for them, and re-layouts, per_device(): design[:, None, :] * design[None, :, :]  10.5 us
  transfers between devices with their start and end apart: 3, of which 3 were waited for; matrix products, arithmetic and copies ran while one was open for 2% of the time, Pallas kernels for 0%

profile of v1, /device:TPU:0, one launch (start us, length us, event | category | flops | bytes accessed | tf_op | source)
XLA Modules:
  0.0 382.6 jit_solution(11348516062546511094)
XLA Ops:
  6.5 1.0 concatenate.6
  7.6 8.0 %broadcast_multiply_fusion = f32[33,33,3072]{2,1,0:T(8,128)} fusion(f32[33,3072]{1,0:T(8,128)S(1)} %concatenate.6), kind=kLoop, calls=%fused_computation.1 | loop fusion | flops 3345408 | bytes 13787136 | tf_op jit(solution)/shard_map/mul | solution.py:46
  15.6 10.5 %mul.11354 = f32[1089,3072]{1,0:T(8,128)} reshape(f32[33,33,3072]{2,1,0:T(8,128)} %broadcast_multiply_fusion) | data formatting | bytes 26763264 | tf_op jit(solution)/shard_map/mul | solution.py:46
  26.1 14.2 %fusion.8 = f32[1089,32]{0,1:T(8,128)S(1)} fusion(f32[1089,3072]{1,0:T(8,128)} %mul.11354, s32[32,3072]{1,0:T(8,128)S(1)} %copy-done.2), kind=kOutput, calls=%fused_computation.548 | convolution fusion | flops 1284734976 | bytes 13914240 | tf_op jit(solution)/shard_map/dot_general | solution.py:47
  40.5 1.2 copy.71
  43.4 42.9 %psum.21 = f32[33,32]{1,0:T(8,128)S(1)} all-reduce(f32[33,32]{1,0:T(8,128)S(1)} %fusion.4), channel_id=1, replica_groups=mesh['rows'=8,'cols'=16] {'rows'}, use_global_device_ids=true, to_apply=%region_0.0 | all-reduce | flops 1056 | bytes 8448 | tf_op jit(solution)/shard_map/psum | solution.py:53
  86.3 44.7 %all-reduce.4.cloned.1.call-done = f32[33,33,32]{2,0,1:T(8,128)} async-done(((f32[33,33,32]{2,0,1:T(8,128)}), f32[33,33,32]{2,0,1:T(8,128)}) %all-reduce.4.cloned.1.call-update) | async-done | bytes 139408 | tf_op jit(solution)/shard_map/psum | solution.py:53
  131.1 0.8 fusion.113
  133.3 0.8 constant_dynamic-update-slice_fusion.454
  135.0 0.8 constant_dynamic-update-slice_fusion.79
  136.7 0.8 constant_dynamic-update-slice_fusion.514
  138.5 0.8 constant_dynamic-update-slice_fusion.513
  149.1 0.8 fusion.144
  150.5 0.8 subtract_divide_fusion
  152.2 3.5 stack.170
  155.7 4.6 %all-to-all-start = ((bf16[16,2,32,3072]{3,2,1,0:T(8,128)(2,1)}), bf16[16,2,32,3072]{3,2,1,0:T(8,128)(2,1)}, u32[]{:S(2)}, u32[]{:S(2)}) async-start(bf16[16,2,32,3072]{3,2,1,0:T(8,128)(2,1)} %stack.170), calls=%async_computation | async-start | bytes 12582912 | tf_op jit(solution)/shard_map/all_to_all | solution.py:71
  160.6 84.1 %all-to-all-done = bf16[16,2,32,3072]{3,2,1,0:T(8,128)(2,1)} async-done(((bf16[16,2,32,3072]{3,2,1,0:T(8,128)(2,1)}), bf16[16,2,32,3072]{3,2,1,0:T(8,128)(2,1)}, u32[]{:S(2)}, u32[]{:S(2)}) %all-to-all-start) | async-done | bytes 6291488 | tf_op jit(solution)/shard_map/all_to_all | solution.py:71
  244.7 3.2 copy.151
  247.9 2.7 copy-done
  250.6 2.5 dynamic-slice_select_fusion
  253.1 5.2 %fusion.1262 = (bf16[1,16,32,3072]{3,2,1,0:T(8,128)(2,1)S(1)}, bf16[1,16,32,3072]{3,2,1,0:T(8,128)(2,1)}) fusion(bf16[2,16,32,3072]{3,2,1,0:T(8,128)(2,1)} %bitcast.7585), kind=kLoop, calls=%fused_computation.3087 | loop fusion | bytes 12582912 | tf_op jit(solution)/shard_map/slice | solution.py:82
  258.3 92.6 %all-reduce.6.cloned.1.call-done = bf16[2,512,1536]{2,1,0:T(8,128)(2,1)} async-done(((bf16[2,512,1536]{2,1,0:T(8,128)(2,1)}), bf16[2,512,1536]{2,1,0:T(8,128)(2,1)}) %all-reduce.6.cloned.1.call-update) | async-done | bytes 3145744 | tf_op jit(solution)/shard_map/psum | solution.py:9
  350.9 11.6 %fusion = f32[3072,1536]{1,0:T(8,128)} fusion(bf16[512,3072]{1,0:T(8,128)(2,1)} %bitcast.7587, bf16[2,512,1536]{2,1,0:T(8,128)(2,1)} %all-reduce.6.cloned.1.call-done), kind=kOutput, calls=%fused_computation.6 | convolution fusion | flops 4831838208 | bytes 23592960 | tf_op jit(solution)/shard_map/dot_general | solution.py:78
  362.6 13.2 %multiply_divide_fusion = f32[3072,1536]{1,0:T(8,128)} fusion(f32[3072,1536]{1,0:T(8,128)} %fusion, bf16[512,3072]{1,0:T(8,128)(2,1)S(1)} %bitcast.7586, bf16[2,512,1536]{2,1,0:T(8,128)(2,1)S(1)} %copy-done.5), kind=kOutput, calls=%fused_computation | convolution fusion | flops 4841275392 | bytes 42467328 | tf_op jit(solution)/shard_map/dot_general | solution.py:81
  (309 shorter events, 16.2 us)
Async XLA Ops:
  6.5 124.5 %all-reduce.4.cloned.1.call-start = ((), (), s32[]{:S(2)}) async-start(), calls=%async_computation.1 | async-start | bytes 1351680 | tf_op jit(solution)/shard_map/psum | solution.py:53
  15.6 10.6 %copy-start.2 = (s32[32,3072]{1,0:T(8,128)S(1)}, s32[32,3072]{1,0:T(8,128)}, u32[]{:S(2)}) copy-start(s32[32,3072]{1,0:T(8,128)} %param.4) | copy-start | bytes 1179652
  26.1 16.0 %copy-start.1 = (f32[32,3072]{1,0:T(8,128)S(1)}, f32[32,3072]{1,0:T(8,128)}, u32[]{:S(2)}) copy-start(f32[32,3072]{1,0:T(8,128)} %param.5) | copy-start | bytes 1179652
  26.1 16.0 %copy-start.4 = (s32[32,3072]{1,0:T(8,128)S(1)}, s32[32,3072]{1,0:T(8,128)}, u32[]{:S(2)}) copy-start(s32[32,3072]{1,0:T(8,128)} %param.3) | copy-start | bytes 1179652
  131.1 9.1 %copy-start.3 = (f32[33,33,32]{2,0,1:T(8,128)S(1)}, f32[33,33,32]{2,0,1:T(8,128)}, u32[]{:S(2)}) copy-start(f32[33,33,32]{2,0,1:T(8,128)} %all-reduce.4.cloned.1.call-done) | copy-start | bytes 418180
  155.7 89.0 %all-to-all-start = ((bf16[16,2,32,3072]{3,2,1,0:T(8,128)(2,1)}), bf16[16,2,32,3072]{3,2,1,0:T(8,128)(2,1)}, u32[]{:S(2)}, u32[]{:S(2)}) async-start(bf16[16,2,32,3072]{3,2,1,0:T(8,128)(2,1)} %stack.170), calls=%async_computation | async-start | bytes 12582912 | tf_op jit(solution)/shard_map/all_to_all | solution.py:71
  160.3 190.6 %all-reduce.6.cloned.1.call-start = ((), (), s32[]{:S(2)}) async-start(), calls=%async_computation.2 | async-start | bytes 6291456 | tf_op jit(solution)/shard_map/psum | solution.py:9
  247.9 2.7 copy-start
  350.9 11.7 %copy-start.5 = (bf16[2,512,1536]{2,1,0:T(8,128)(2,1)S(1)}, bf16[2,512,1536]{2,1,0:T(8,128)(2,1)}, u32[]{:S(2)}) copy-start(bf16[2,512,1536]{2,1,0:T(8,128)(2,1)} %all-reduce.6.cloned.1.call-done) | copy-start | bytes 9437188
Sparse Core Ops, SparseCore 0:
  41.9 89.1 all-reduce.3
  253.2 97.6 all-reduce.5

commit v2 on v0

--- a/solution.py
+++ b/solution.py
@@ -2,11 +2,12 @@
 import jax.numpy as jnp
 from jax import lax
 from jax.sharding import PartitionSpec as P
+from jax.lax import all_gather
 
 
 def broadcast(block, axis, holder):
     block = jnp.where(lax.axis_index(axis) == holder, block, jnp.zeros_like(block))
-    return lax.psum(block, axis)
+    return jnp.sum(all_gather(block, axis), 0)
 
 
 def solve_normal(gram, moment):

time: 340 us -> 516 us (1.52)
  waiting for transfers between devices: 186 us -> 348 us
  other arithmetic: 37.7 us -> 51.5 us
    all_gather x0 -> x1, waiting for transfers between devices: none -> 263 us  [broadcast(): return jnp.sum(all_gather(block, axis), 0)]
    psum x1 -> x0, waiting for transfers between devices: 101 us -> none  [broadcast(): return lax.psum(block, axis)]
    reduce_sum x0 -> x1, other arithmetic: none -> 13.8 us  [broadcast(): return jnp.sum(all_gather(block, axis), 0)]
where the time goes in v2:
time: 516 us; the launch traced here: 515 us
  waiting for transfers between devices  348 us (67%)
  other arithmetic  51.5 us (10%)
  blocking collectives  42.9 us (8%)
  matrix products  41.1 us (8%)
  local copies, waits for them, and re-layouts  16.1 us (3%)
  between operations  14.6 us (3%)
    all_gather x1, waiting for transfers between devices, broadcast(): return jnp.sum(all_gather(block, axis), 0)  263 us
    psum x1, waiting for transfers between devices, per_device(): gram_flat, moment = lax.psum((gram_part, moment_part), 'rows')  44.7 us
    psum x1, blocking collectives, per_device(): gram_flat, moment = lax.psum((gram_part, moment_part), 'rows')  42.9 us
    all_gather x1, waiting for transfers between devices, per_device(): full_rows = lax.all_gather(panel, 'cols', axis=1, tiled=True)  40.2 us
    dot_general x1, matrix products, per_device(): lax.dot_general(full_rows[1], full_cols[1], contract, preferred_element_t...  14.2 us
    dot_general x1, matrix products, per_device(): jnp.dot(outer_rows, observed.T, precision=lax.Precision.HIGHEST, preferre...  14.2 us
    reduce_sum x1, other arithmetic, broadcast(): return jnp.sum(all_gather(block, axis), 0)  13.8 us
    dot_general x1, matrix products, per_device(): lax.dot_general(full_rows[0], full_cols[0], contract, preferred_element_t...  11.4 us
  transfers between devices with their start and end apart: 3, of which 3 were waited for; matrix products, arithmetic and copies ran while one was open for 0% of the time, Pallas kernels for 0%

profile of v2, /device:TPU:0, one launch (start us, length us, event | category | flops | bytes accessed | tf_op | source)
XLA Modules:
  0.0 514.9 jit_solution(12552472655689058030)
XLA Ops:
  6.5 1.0 concatenate.3
  7.6 8.0 %broadcast_multiply_fusion = f32[33,33,3072]{2,1,0:T(8,128)} fusion(f32[33,3072]{1,0:T(8,128)S(1)} %concatenate.3), kind=kLoop, calls=%fused_computation.1 | loop fusion | flops 3345408 | bytes 13787136 | tf_op jit(solution)/shard_map/mul | solution.py:47
  15.6 10.5 %mul.11354 = f32[1089,3072]{1,0:T(8,128)} reshape(f32[33,33,3072]{2,1,0:T(8,128)} %broadcast_multiply_fusion) | data formatting | bytes 26763264 | tf_op jit(solution)/shard_map/mul | solution.py:47
  26.1 14.2 %fusion.8 = f32[1089,32]{0,1:T(8,128)S(1)} fusion(f32[1089,3072]{1,0:T(8,128)} %mul.11354, s32[32,3072]{1,0:T(8,128)S(1)} %copy-done.1), kind=kOutput, calls=%fused_computation.550 | convolution fusion | flops 1284734976 | bytes 13914240 | tf_op jit(solution)/shard_map/dot_general | solution.py:48
  40.5 1.2 copy.70
  43.4 42.9 %psum.14 = f32[33,32]{1,0:T(8,128)S(1)} all-reduce(f32[33,32]{1,0:T(8,128)S(1)} %fusion.4), channel_id=1, replica_groups=mesh['rows'=8,'cols'=16] {'rows'}, use_global_device_ids=true, to_apply=%region_0.0 | all-reduce | flops 1056 | bytes 8448 | tf_op jit(solution)/shard_map/psum | solution.py:54
  86.4 44.7 %all-reduce.3.cloned.1.call-done = f32[33,33,32]{2,0,1:T(8,128)} async-done(((f32[33,33,32]{2,0,1:T(8,128)}), f32[33,33,32]{2,0,1:T(8,128)}) %all-reduce.3.cloned.1.call-update) | async-done | bytes 139408 | tf_op jit(solution)/shard_map/psum | solution.py:54
  135.0 0.8 constant_dynamic-update-slice_fusion.79
  136.7 0.8 constant_dynamic-update-slice_fusion.514
  138.4 0.8 constant_dynamic-update-slice_fusion.513
  140.1 0.8 constant_dynamic-update-slice_fusion.512
  141.8 0.8 constant_dynamic-update-slice_fusion.511
  143.5 0.8 constant_dynamic-update-slice_fusion.510
  145.2 0.8 constant_dynamic-update-slice_fusion.509
  146.9 0.8 constant_dynamic-update-slice_fusion.508
  148.6 0.8 constant_dynamic-update-slice_fusion.507
  157.1 0.8 fusion.144
  158.4 0.8 subtract_divide_fusion
  161.2 40.2 %all-gather.4.cloned.1.call-done = bf16[2,512,3072]{2,1,0:T(8,128)(2,1)} async-done(((bf16[2,32,3072]{2,1,0:T(8,128)(2,1)}), bf16[2,512,3072]{2,1,0:T(8,128)(2,1)}) %all-gather.4.cloned.1.call-update) | async-done | bytes 6291472 | tf_op jit(solution)/shard_map/all_gather | solution.py:71
  201.4 4.1 dynamic-slice_select_fusion
  205.5 263.4 %all-gather.6.cloned.1.call-done = bf16[16,512,1536]{2,1,0:T(8,128)(2,1)} async-done(((bf16[2,512,1536]{2,1,0:T(8,128)(2,1)}), bf16[16,512,1536]{2,1,0:T(8,128)(2,1)}) %all-gather.6.cloned.1.call-update) | async-done | bytes 25165840 | tf_op jit(solution)/shard_map/all_gather | solution.py:10
  468.9 13.8 %reduce_sum.416 = bf16[2,512,1536]{2,1,0:T(8,128)(2,1)S(1)} reduce(bf16[8,2,512,1536]{3,2,1,0:T(8,128)(2,1)} %bitcast.7583, bf16[]{:T(256)} %constant.119.clone.1), dimensions={0}, to_apply=%region_33.34 | reduce | flops 11010048 | bytes 28311554 | tf_op jit(solution)/shard_map/reduce_sum | solution.py:10
  482.7 11.4 %fusion = f32[3072,1536]{1,0:T(8,128)} fusion(bf16[2,512,3072]{2,1,0:T(8,128)(2,1)} %all-gather.4.cloned.1.call-done, bf16[2,512,1536]{2,1,0:T(8,128)(2,1)S(1)} %reduce_sum.416), kind=kOutput, calls=%fused_computation.5 | convolution fusion | flops 4831838208 | bytes 23592960 | tf_op jit(solution)/shard_map/dot_general | solution.py:74
  494.2 14.2 %multiply_divide_fusion = f32[3072,1536]{1,0:T(8,128)} fusion(f32[3072,1536]{1,0:T(8,128)} %fusion, bf16[2,512,3072]{2,1,0:T(8,128)(2,1)} %all-gather.4.cloned.1.call-done, bf16[2,512,1536]{2,1,0:T(8,128)(2,1)S(1)} %reduce_sum.416), kind=kOutput, calls=%fused_computation | convolution fusion | flops 4841275392 | bytes 42467328 | tf_op jit(solution)/shard_map/dot_general | solution.py:77
  (304 shorter events, 21.7 us)
Async XLA Ops:
  6.5 124.5 %all-reduce.3.cloned.1.call-start = ((), (), s32[]{:S(2)}) async-start(), calls=%async_computation | async-start | bytes 1351680 | tf_op jit(solution)/shard_map/psum | solution.py:54
  15.6 10.6 %copy-start.1 = (s32[32,3072]{1,0:T(8,128)S(1)}, s32[32,3072]{1,0:T(8,128)}, u32[]{:S(2)}) copy-start(s32[32,3072]{1,0:T(8,128)} %param.4) | copy-start | bytes 1179652
  26.1 16.1 %copy-start = (f32[32,3072]{1,0:T(8,128)S(1)}, f32[32,3072]{1,0:T(8,128)}, u32[]{:S(2)}) copy-start(f32[32,3072]{1,0:T(8,128)} %param.5) | copy-start | bytes 1179652
  26.1 16.1 %copy-start.3 = (s32[32,3072]{1,0:T(8,128)S(1)}, s32[32,3072]{1,0:T(8,128)}, u32[]{:S(2)}) copy-start(s32[32,3072]{1,0:T(8,128)} %param.3) | copy-start | bytes 1179652
  41.8 159.6 %all-gather.4.cloned.1.call-start = ((), (), s32[]{:S(2)}) async-start(), calls=%async_computation.1 | async-start | bytes 6684672 | tf_op jit(solution)/shard_map/all_gather | solution.py:71
  131.0 18.4 %copy-start.2 = (f32[33,33,32]{2,0,1:T(8,128)S(1)}, f32[33,33,32]{2,0,1:T(8,128)}, u32[]{:S(2)}) copy-start(f32[33,33,32]{2,0,1:T(8,128)} %all-reduce.3.cloned.1.call-done) | copy-start | bytes 418180
  160.9 308.1 %all-gather.6.cloned.1.call-start = ((), (), s32[]{:S(2)}) async-start(), calls=%async_computation.2 | async-start | bytes 28311552 | tf_op jit(solution)/shard_map/all_gather | solution.py:10
Sparse Core Ops, SparseCore 0:
  41.9 89.0 all-reduce.2
  161.0 40.3 all-gather.3
  205.6 263.2 all-gather.5
